TPU v7x, 512 devices: a whole 4x4x16 slice. The times are simulated.
512 devices in a mesh: snp: 32 (over y, x, core), ind: 16 (over z).
Axes of the slice: x: 4, y: 4, z: 16, core: 2. Of those that a mesh axis runs over, the one named last changes fastest.
Arguments:
- genotypes: bfloat16 [32768, 16384], P('ind', 'snp'), may hold values from -12 to 12, as said below
- annotations: bfloat16 [16384, 512], P('snp'), may hold values from -0.3984375 to 0.3984375
- window_start: int32 [16384], P(('snp', 'ind')), may hold values from 0 to 16383, as said below
- window_end: int32 [16384], P(('snp', 'ind')), may hold values from 1 to 16384, as said below
Outputs:
- ld_scores: float32 [16384, 512], P(('snp', 'ind'))
Inputs may be any that keep to these rules, and one draw needn't show every extreme that they name: `genotypes`: real-valued dosages, each SNP with its own scale; values within the range. For each SNP j: window_start(j) <= j; j - window_start(j) <= 512, reached on every draw; k is in the window of j exactly when j is in the window of k; never falls along the SNPs. For each SNP j: window_end(j) > j; window_end(j) - j <= 513, reached on every draw; never falls along the SNPs.
All inputs are finite; a program needn't handle non-finite values.
Results may differ from a plain program's by a relative error of at most 0.0033.
Values may be sent and summed in bfloat16 or wider, within the bound.
A program may use at most 64 MiB of HBM per device.

v0:
```python
import jax
import jax.numpy as jnp
from jax import lax
from jax.sharding import PartitionSpec as P


def extended(cells, sides, width):
    for axis, dim in sides:
        count = lax.axis_size(axis)
        ends = count - 1
        head = lax.slice_in_dim(cells, 0, width, axis=dim)
        tail = lax.slice_in_dim(cells, cells.shape[dim] - width, cells.shape[dim], axis=dim)
        cells = jnp.concatenate(
            [
                lax.ppermute(tail, axis, [(i, (i + 1) % count) for i in range(ends)]),
                cells,
                lax.ppermute(head, axis, [((i + 1) % count, i) for i in range(ends)]),
            ],
            axis=dim,
        )
    return cells


def gathered_total(array, axis):
    parts = lax.all_gather(array, axis)
    return parts.sum(axis=0)


def adjust_block(gram_tile, row_sumsq, col_sumsq, col_ids, start_rows, end_rows, count_all):
    col_safe = jnp.where(col_sumsq > 0.0, col_sumsq, 1.0)
    corr_value = gram_tile * lax.rsqrt(row_sumsq)[:, None] * lax.rsqrt(col_safe)[None, :]
    squared = corr_value * corr_value
    adjusted = squared - (1.0 - squared) / (count_all - 2.0)
    inside = (col_ids[None, :] >= start_rows[:, None]) & (col_ids[None, :] < end_rows[:, None])
    return jnp.where(inside, adjusted, 0.0).astype(jnp.bfloat16)


def column_squares(block):
    widened = block.astype(jnp.float32)
    return jnp.sum(widened * widened, axis=0)


def transposed_product(left, right):
    return lax.dot_general(
        left, right, (((0,), (0,)), ((), ())), preferred_element_type=jnp.float32
    )


def per_device(genotypes, annotations, window_start, window_end):
    stripe = genotypes.shape[1]
    groups = lax.axis_size("ind")
    count_all = float(genotypes.shape[0] * groups)
    sub_rows = stripe // groups
    row_lead = lax.axis_index("ind") * sub_rows
    stripe_first = lax.axis_index("snp") * stripe
    wide_geno = extended(genotypes, (("snp", 1),), stripe)
    wide_annot = extended(annotations, (("snp", 0),), stripe)
    col_first = stripe_first - stripe
    gram_tile = lax.psum_scatter(
        transposed_product(genotypes, wide_geno), "ind", scatter_dimension=0, tiled=True
    )
    col_sumsq = gathered_total(column_squares(wide_geno), "ind")
    row_sumsq = lax.dynamic_slice_in_dim(col_sumsq, stripe + row_lead, sub_rows, 0)
    col_ids = col_first + jnp.arange(wide_geno.shape[1], dtype=jnp.int32)
    weights = adjust_block(
        gram_tile, row_sumsq, col_sumsq, col_ids, window_start, window_end, count_all
    )
    own_score = jnp.dot(weights, wide_annot, preferred_element_type=jnp.float32)
    return own_score


def solution(mesh):
    in_specs = (P("ind", "snp"), P("snp", None), P(("snp", "ind")), P(("snp", "ind")))
    out_specs = P(("snp", "ind"), None)
    return jax.shard_map(
        per_device, mesh=mesh, in_specs=in_specs, out_specs=out_specs, check_vma=False
    )
```

profile of v0, /device:TPU:24, one launch (start us, length us, event | category | flops | bytes accessed | tf_op | source)
XLA Modules:
  0.0 139.1 jit_solution(8316424443001831641)
XLA Ops:
  6.5 0.0 copy-start.1
  6.5 0.0 reduce-scatter.4.cloned.1.call-start
  6.5 2.0 %collective-permute-start = (bf16[2048,512]{1,0:T(8,128)(2,1)}, bf16[2048,512]{1,0:T(8,128)(2,1)S(1)}, u32[]{:S(2)}, u32[]{:S(2)}) collective-permute-start(bf16[2048,512]{1,0:T(8,128)(2,1)} %param.4), channel_id=1, source_target_pairs={{0,16},{16,32},{32,48},{48,64},{64,80},{80,96},{96,112},{112,128},... | collective-permute-start | bytes 6291464 | tf_op jit(solution)/shard_map/ppermute | solution.py:15
  8.6 5.8 %collective-permute-start.1 = (bf16[2048,512]{1,0:T(8,128)(2,1)}, bf16[2048,512]{1,0:T(8,128)(2,1)S(1)}, u32[]{:S(2)}, u32[]{:S(2)}) collective-permute-start(bf16[2048,512]{1,0:T(8,128)(2,1)} %param.4), channel_id=1, source_target_pairs={{16,0},{32,16},{48,32},{64,48},{80,64},{96,80},{112,96},{128,112},... | collective-permute-start | bytes 6291464 | tf_op jit(solution)/shard_map/ppermute | solution.py:17
  14.4 22.0 %collective-permute-done = bf16[2048,512]{1,0:T(8,128)(2,1)S(1)} collective-permute-done((bf16[2048,512]{1,0:T(8,128)(2,1)}, bf16[2048,512]{1,0:T(8,128)(2,1)S(1)}, u32[]{:S(2)}, u32[]{:S(2)}) %collective-permute-start) | collective-permute-done | bytes 2097184 | tf_op jit(solution)/shard_map/ppermute | solution.py:15
  36.3 0.1 constant_dynamic-update-slice_fusion.2
  36.5 0.0 copy-done.1
  36.5 0.0 copy-start.2
  36.5 0.1 constant_dynamic-update-slice_fusion.1
  36.6 1.6 %collective-permute-done.1 = bf16[2048,512]{1,0:T(8,128)(2,1)S(1)} collective-permute-done((bf16[2048,512]{1,0:T(8,128)(2,1)}, bf16[2048,512]{1,0:T(8,128)(2,1)S(1)}, u32[]{:S(2)}, u32[]{:S(2)}) %collective-permute-start.1) | collective-permute-done | bytes 2097184 | tf_op jit(solution)/shard_map/ppermute | solution.py:17
  38.2 0.1 constant_dynamic-update-slice_fusion
  38.3 0.0 copy-start
  38.3 2.6 %copy-done = bf16[2048,1536]{1,0:T(8,128)(2,1)} copy-done((bf16[2048,1536]{1,0:T(8,128)(2,1)}, bf16[2048,1536]{1,0:T(8,128)(2,1)S(1)}, u32[]{:S(2)}) %copy-start) | copy-done | bytes 6291480
  41.0 0.0 copy-done.2
  41.0 3.5 %convolution_bitcast_fusion = f32[512,1536]{0,1:T(8,128)S(1)} fusion(bf16[2048,1536]{1,0:T(8,128)(2,1)S(1)} %constant_dynamic-update-slice_fusion, bf16[2048,512]{1,0:T(8,128)(2,1)S(1)} %copy-done.2), kind=kOutput, calls=%fused_computation.1 | convolution fusion | flops 3221225472 | bytes 11534336 | tf_op jit(solution)/shard_map/dot_general | solution.py:44
  44.5 2.4 %copy.5 = f32[512,1536]{1,0:T(8,128)} copy(f32[512,1536]{0,1:T(8,128)S(1)} %convolution_bitcast_fusion) | data formatting | bytes 6291456
  46.9 0.0 copy-start.3
  46.9 0.0 reduce-scatter.4.cloned.1.call-update
  46.9 1.0 copy-done.3
  47.9 1.9 %collective-permute-start.2 = (bf16[512,512]{1,0:T(8,128)(2,1)S(1)}, bf16[512,512]{1,0:T(8,128)(2,1)S(1)}, u32[]{:S(2)}, u32[]{:S(2)}) collective-permute-start(bf16[512,512]{1,0:T(8,128)(2,1)S(1)} %copy-done.3), channel_id=1, source_target_pairs={{0,16},{16,32},{32,48},{48,64},{64,80},{80,96},{96,112},{112,128},... | collective-permute-start | bytes 1572872 | tf_op jit(solution)/shard_map/ppermute | solution.py:15
  49.8 5.8 %collective-permute-start.3 = (bf16[512,512]{1,0:T(8,128)(2,1)S(1)}, bf16[512,512]{1,0:T(8,128)(2,1)S(1)}, u32[]{:S(2)}, u32[]{:S(2)}) collective-permute-start(bf16[512,512]{1,0:T(8,128)(2,1)S(1)} %copy-done.3), channel_id=1, source_target_pairs={{16,0},{32,16},{48,32},{64,48},{80,64},{96,80},{112,96},{128,112},... | collective-permute-start | bytes 1572872 | tf_op jit(solution)/shard_map/ppermute | solution.py:17
  55.7 0.0 copy-start.4
  55.7 0.0 copy-start.5
  55.7 4.1 %multiply_reduce_fusion = f32[1536]{0:T(1024)S(1)} fusion(bf16[2048,1536]{1,0:T(8,128)(2,1)} %copy-done), kind=kLoop, calls=%fused_computation | loop fusion | flops 9435648 | bytes 6297600 | tf_op jit(solution)/shard_map/reduce_sum | solution.py:40
  59.8 35.9 %all-gather.1 = f32[16,1,1536]{2,1,0:T(1,128)S(1)} all-gather(f32[1,1,1536]{2,1,0:T(1,128)S(1)} %reshape.13), channel_id=2, replica_groups=mesh['snp'=32,'ind'=16] {'ind'}, dimensions={0}, use_global_device_ids=true | all-gather | bytes 104448 | tf_op jit(solution)/shard_map/all_gather | solution.py:25
  95.7 0.1 reduce_sum.19
  95.8 0.1 dynamic-slice_rsqrt_fusion
  95.9 33.6 %reduce-scatter.4.cloned.1.call-done = f32[32,1536]{1,0:T(8,128)} async-done(((f32[512,1536]{1,0:T(8,128)}), f32[32,1536]{1,0:T(8,128)}) %reduce-scatter.4.cloned.1.call-update) | async-done | bytes 196624
  129.5 1.2 copy.6
  130.7 0.0 collective-permute-done.2
  130.7 0.0 collective-permute-done.3
  130.7 0.0 copy-done.4
  130.7 0.0 copy-done.5
  130.7 1.5 %fusion = f32[32,512]{1,0:T(8,128)} fusion(bf16[512,512]{1,0:T(8,128)(2,1)S(1)} %collective-permute-done.3, bf16[512,512]{1,0:T(8,128)(2,1)S(1)} %copy-done.3, bf16[512,512]{1,0:T(8,128)(2,1)S(1)} %collective-permute-done.2, f32[32,1536]{0,1:T(8,128)S(1)} %copy.6, f32[1536]{0:T(1024)S(1)} %fusion.14, f32[32]{0:T(128)S(1)} %dynamic-slice_rsqrt_fusion, ...), kind=kOutput, calls=%fused_computation.2 | convolution fusion | flops 55590912 | bytes 1847680 | tf_op jit(solution)/shard_map/dot_general | solution.py:68
  (3 shorter events, 0.0 us)
Async XLA Ops:
  6.5 29.9 %copy-start.1 = (bf16[2048,512]{1,0:T(8,128)(2,1)S(1)}, bf16[2048,512]{1,0:T(8,128)(2,1)}, u32[]{:S(2)}) copy-start(bf16[2048,512]{1,0:T(8,128)(2,1)} %param.4) | copy-start | bytes 6291460
  6.5 122.9 %reduce-scatter.4.cloned.1.call-start = ((), (), s32[]{:S(2)}) async-start(), calls=%async_computation.1 | async-start | bytes 3342336
  6.5 29.8 %collective-permute-start = (bf16[2048,512]{1,0:T(8,128)(2,1)}, bf16[2048,512]{1,0:T(8,128)(2,1)S(1)}, u32[]{:S(2)}, u32[]{:S(2)}) collective-permute-start(bf16[2048,512]{1,0:T(8,128)(2,1)} %param.4), channel_id=1, source_target_pairs={{0,16},{16,32},{32,48},{48,64},{64,80},{80,96},{96,112},{112,128},... | collective-permute-start | bytes 6291464 | tf_op jit(solution)/shard_map/ppermute | solution.py:15
  8.6 29.6 %collective-permute-start.1 = (bf16[2048,512]{1,0:T(8,128)(2,1)}, bf16[2048,512]{1,0:T(8,128)(2,1)S(1)}, u32[]{:S(2)}, u32[]{:S(2)}) collective-permute-start(bf16[2048,512]{1,0:T(8,128)(2,1)} %param.4), channel_id=1, source_target_pairs={{16,0},{32,16},{48,32},{64,48},{80,64},{96,80},{112,96},{128,112},... | collective-permute-start | bytes 6291464 | tf_op jit(solution)/shard_map/ppermute | solution.py:17
  36.5 4.5 %copy-start.2 = (bf16[2048,512]{1,0:T(8,128)(2,1)S(1)}, bf16[2048,512]{1,0:T(8,128)(2,1)}, u32[]{:S(2)}) copy-start(bf16[2048,512]{1,0:T(8,128)(2,1)} %param.4) | copy-start | bytes 6291460
  38.3 2.7 %copy-start = (bf16[2048,1536]{1,0:T(8,128)(2,1)}, bf16[2048,1536]{1,0:T(8,128)(2,1)S(1)}, u32[]{:S(2)}) copy-start(bf16[2048,1536]{1,0:T(8,128)(2,1)S(1)} %constant_dynamic-update-slice_fusion) | copy-start | bytes 18874372
  46.9 1.0 copy-start.3
  47.9 82.8 %collective-permute-start.2 = (bf16[512,512]{1,0:T(8,128)(2,1)S(1)}, bf16[512,512]{1,0:T(8,128)(2,1)S(1)}, u32[]{:S(2)}, u32[]{:S(2)}) collective-permute-start(bf16[512,512]{1,0:T(8,128)(2,1)S(1)} %copy-done.3), channel_id=1, source_target_pairs={{0,16},{16,32},{32,48},{48,64},{64,80},{80,96},{96,112},{112,128},... | collective-permute-start | bytes 1572872 | tf_op jit(solution)/shard_map/ppermute | solution.py:15
  49.8 80.9 %collective-permute-start.3 = (bf16[512,512]{1,0:T(8,128)(2,1)S(1)}, bf16[512,512]{1,0:T(8,128)(2,1)S(1)}, u32[]{:S(2)}, u32[]{:S(2)}) collective-permute-start(bf16[512,512]{1,0:T(8,128)(2,1)S(1)} %copy-done.3), channel_id=1, source_target_pairs={{16,0},{32,16},{48,32},{64,48},{80,64},{96,80},{112,96},{128,112},... | collective-permute-start | bytes 1572872 | tf_op jit(solution)/shard_map/ppermute | solution.py:17
  55.7 75.0 %copy-start.4 = (s32[32]{0:T(128)S(1)}, s32[32]{0:T(128)}, u32[]{:S(2)}) copy-start(s32[32]{0:T(128)} %param.7) | copy-start | bytes 388
  55.7 75.0 %copy-start.5 = (s32[32]{0:T(128)S(1)}, s32[32]{0:T(128)}, u32[]{:S(2)}) copy-start(s32[32]{0:T(128)} %param.6) | copy-start | bytes 388
Sparse Core Ops, SparseCore 0:
  47.0 82.4 reduce-scatter.3
where the time goes:
time: 140 us; the launch traced here: 139 us
  waiting for transfers between devices  57.2 us (41%)
  blocking collectives  35.9 us (26%)
  starting transfers between devices  15.5 us (11%)
  between operations  13.5 us (10%)
  local copies, waits for them, and re-layouts  7.77 us (6%)
  matrix products  5 us (4%)
  other arithmetic  4.17 us (3%)
    all_gather x1, blocking collectives, gathered_total(): parts = lax.all_gather(array, axis)  35.9 us
    unnamed x2, waiting for transfers between devices  33.6 us
    ppermute x2, waiting for transfers between devices, extended(): lax.ppermute(tail, axis, [(i, (i + 1) % count) for i in range(ends)])  22 us
    ppermute x2, starting transfers between devices, extended(): lax.ppermute(head, axis, [((i + 1) % count, i) for i in range(ends)])  11.6 us
    unnamed x17, local copies, waits for them, and re-layouts  7.55 us
    reduce_sum x1, other arithmetic, column_squares(): return jnp.sum(widened * widened, axis=0)  4.1 us
    ppermute x2, starting transfers between devices, extended(): lax.ppermute(tail, axis, [(i, (i + 1) % count) for i in range(ends)])  3.95 us
    dot_general x1, matrix products, transposed_product(): lax.dot_general(left, right, (((0,), (0,)), ((), ())), preferred_element_...  3.46 us
  transfers between devices with their start and end apart: 5, of which 3 were waited for; matrix products, arithmetic and copies ran while one was open for 4% of the time, Pallas kernels for 0%

commit v1 on v0

v1 whole, which is shorter than its diff:
```python
import functools

import jax
import jax.numpy as jnp
from jax import lax
from jax.experimental import pallas as pl
from jax.experimental.pallas import tpu as pltpu
from jax.sharding import PartitionSpec as P

MESH = pl.DeviceIdType.MESH
BF16, F32 = jnp.bfloat16, jnp.float32


def tdot(left, right):
    return lax.dot_general(left, right, (((0,), (0,)), ((), ())), preferred_element_type=F32)


def mm(left, right):
    return jnp.dot(left, right, preferred_element_type=F32)


def safe_rsqrt(v):
    return lax.rsqrt(jnp.where(v > 0.0, v, 1.0))


def kernel(count_all, snps, geno, annot, first, last, out,
           x_v, l0, r1, a_own, a_prev, a_next,
           s1, s2, s3, g1, g2, g3, ss_own, ss_all, ss_tot, ss_side,
           p1, p2, p3, t1, t2, t3,
           x_sem, a_sem, halo_send, halo_recv, ring,
           ss_send, ss_recv, side_send, side_recv,
           g_send, g_recv1, g_recv2, g_recv3, t_send, t_recv1, t_recv2, t_recv3):
    s = lax.axis_index("snp")
    z = lax.axis_index("ind")
    ns, nz = snps, 16
    right, left = lax.rem(s + 1, ns), lax.rem(s + ns - 1, ns)

    def zpeer(d):
        return lax.rem(z + d + nz, nz)

    def rcopy(src, dst, ssem, rsem, dev):
        return pltpu.make_async_remote_copy(
            src_ref=src, dst_ref=dst, send_sem=ssem, recv_sem=rsem,
            device_id=dev, device_id_type=MESH)

    def signal(sem, dev):
        pl.semaphore_signal(sem, inc=1, device_id=dev, device_id_type=MESH)

    x_copy = pltpu.make_async_copy(geno, x_v, x_sem)
    x_copy.start()
    a_copy = pltpu.make_async_copy(annot, a_own, a_sem)
    a_copy.start()

    barrier = pltpu.get_barrier_semaphore()
    signal(barrier, {"snp": left})
    signal(barrier, {"snp": right})
    signal(barrier, {"ind": zpeer(1)})
    signal(barrier, {"ind": zpeer(-1)})
    pl.semaphore_wait(barrier, 4)

    h_left = rcopy(geno.at[:, pl.ds(0, 256)], l0, halo_send.at[0], halo_recv.at[0], {"snp": left})
    h_right = rcopy(geno.at[:, pl.ds(256, 256)], r1, halo_send.at[1], halo_recv.at[1], {"snp": right})
    h_left.start()
    h_right.start()
    ann_l = rcopy(annot, a_next, halo_send.at[2], halo_recv.at[2], {"snp": left})
    ann_r = rcopy(annot, a_prev, halo_send.at[3], halo_recv.at[3], {"snp": right})
    ann_l.start()
    ann_r.start()

    signal(ring.at[0], {"ind": zpeer(1)})
    signal(ring.at[0], {"ind": zpeer(-1)})

    eye = (lax.broadcasted_iota(jnp.int32, (256, 256), 0)
           == lax.broadcasted_iota(jnp.int32, (256, 256), 1))

    x_copy.wait()
    m_lo = tdot(x_v[:, 0:256], x_v[...])
    for b in range(4):
        s1[0:8, b] = m_lo[:, 128 * b:128 * b + 128].reshape(8, 32, 128).astype(BF16)
    ss_own[:, 0:256] = jnp.sum(jnp.where(eye, m_lo[:, 0:256], 0.0), axis=0, keepdims=True)
    pl.semaphore_wait(ring.at[0], 2)
    signal(ring.at[1], {"ind": zpeer(2)})
    signal(ring.at[1], {"ind": zpeer(-2)})
    m_hi = tdot(x_v[:, 256:512], x_v[:, 256:512])
    for b in range(2):
        s1[8:16, 2 + b] = m_hi[:, 128 * b:128 * b + 128].reshape(8, 32, 128).astype(BF16)
    ss_own[:, 256:512] = jnp.sum(jnp.where(eye, m_hi, 0.0), axis=0, keepdims=True)
    pl.semaphore_wait(ring.at[1], 2)
    signal(ring.at[2], {"ind": zpeer(4)})
    signal(ring.at[2], {"ind": zpeer(-4)})
    pl.semaphore_wait(ring.at[2], 2)

    def ss_copy(d):
        dest = lax.rem(z + d, nz)
        return rcopy(ss_own, ss_all.at[z], ss_send.at[d], ss_recv.at[z], {"ind": dest})

    def each_peer(body):
        def step(d, carry):
            body(d)
            return carry
        lax.fori_loop(1, nz, step, 0)

    each_peer(lambda d: ss_copy(d).start())

    def g1_pieces(i, act):
        for g in range(4):
            @pl.when(i // 4 == g)
            def _():
                act(pl.ds(g, 4 - g))

    def g2_pieces(i, act):
        @pl.when(i < 4)
        def _():
            act(pl.ds(0, 1))

        @pl.when(i >= 4)
        def _():
            act(pl.ds(0, 2))

    def g3_pieces(i, act):
        @pl.when((i >= 8) & (i < 12))
        def _():
            act(pl.ds(0, 2))

        @pl.when(i >= 12)
        def _():
            act(pl.ds(1, 1))

    groups = ((s1, g1, g_recv1, g1_pieces, 0), (s2, g2, g_recv2, g2_pieces, 0), (s3, g3, g_recv3, g3_pieces, 8))

    def part_copy(k, d, part):
        src, dst, rsem, _, base = groups[k]
        dest = lax.rem(z + d, nz)
        return rcopy(src.at[dest - base, part], dst.at[z, part], g_send.at[k, d], rsem.at[z], {"ind": dest})

    def part_start(k):
        def body(d):
            groups[k][3](lax.rem(z + d, nz), lambda part: part_copy(k, d, part).start())
        each_peer(body)

    def part_send_wait(k):
        def body(d):
            groups[k][3](lax.rem(z + d, nz), lambda part: part_copy(k, d, part).wait_send())
        each_peer(body)

    def part_recv_wait(k):
        src, dst, rsem, pieces, base = groups[k]

        def body(d):
            origin = lax.rem(z + d, nz)
            pieces(z, lambda part: rcopy(
                dst.at[origin, part], dst.at[origin, part], g_send.at[k, d], rsem.at[origin], {"ind": origin}).wait_recv())
        each_peer(body)

    part_start(0)

    def next_part():
        h_left.wait_recv()
        m2 = tdot(x_v[...], l0[...])
        for b in range(2):
            s2[:, b] = m2[:, 128 * b:128 * b + 128].reshape(16, 32, 128).astype(BF16)
        part_start(1)

    def prev_part():
        h_right.wait_recv()
        m3 = tdot(x_v[:, 256:512], r1[...])
        for b in range(2):
            s3[:, b] = m3[:, 128 * b:128 * b + 128].reshape(8, 32, 128).astype(BF16)
        part_start(2)

    @pl.when(lax.rem(s, 2) == 1)
    def _():
        prev_part()

    next_part()

    @pl.when(lax.rem(s, 2) == 0)
    def _():
        prev_part()

    ss_all[z] = ss_own[...]

    def ss_wait(d):
        origin = lax.rem(z + d, nz)
        rcopy(ss_own, ss_all.at[origin], ss_send.at[d], ss_recv.at[origin], {"ind": origin}).wait_recv()
    each_peer(ss_wait)
    ss_tot[...] = jnp.sum(ss_all[...], axis=0)
    side_l = rcopy(ss_tot, ss_side.at[1], side_send.at[0], side_recv.at[1], {"snp": left})
    side_r = rcopy(ss_tot, ss_side.at[0], side_send.at[1], side_recv.at[0], {"snp": right})
    side_l.start()
    side_r.start()

    def column(row, offset):
        n = row.shape[1]
        hit = (lax.broadcasted_iota(jnp.int32, (32, n), 1)
               == lax.broadcasted_iota(jnp.int32, (32, n), 0) + offset)
        return jnp.sum(jnp.where(hit, jnp.broadcast_to(row, (32, n)), jnp.zeros((), row.dtype)),
                       axis=1, keepdims=True)

    lead = z * 32
    low = column(first[...], 0)
    high = column(last[...], 0)
    row_scale = safe_rsqrt(column(ss_tot[...], lead))

    def weigh(gram, col_ss, col_first, keep):
        n = gram.shape[1]
        corr = gram * row_scale * safe_rsqrt(col_ss)
        squared = corr * corr
        adjusted = squared - (1.0 - squared) / (count_all - 2.0)
        ids = lax.broadcasted_iota(jnp.int32, (32, n), 1) + col_first
        inside = (ids >= low) & (ids < high) & keep
        return jnp.where(inside, adjusted, 0.0).astype(BF16).astype(F32)

    def summed(k, width):
        src, dst, _, pieces, base = groups[k]
        total = dst[0].astype(F32)
        for i in range(1, nz):
            total = total + dst[i].astype(F32)
        return jnp.concatenate([total[b] for b in range(width)], axis=1)

    lane = lax.broadcasted_iota(jnp.int32, (8, 128), 1) // 32

    def pack(weights, buf):
        for b in range(weights.shape[1] // 128):
            for u in range(4):
                tile = jnp.zeros((8, 128), F32)
                for v in range(4):
                    piece = weights[8 * v:8 * v + 8, 128 * b:128 * b + 128]
                    shift = (32 * (v - u)) % 128
                    if shift:
                        piece = pltpu.roll(piece, shift, 1)
                    tile = jnp.where(lane == v, piece, tile)
                buf[4 * b + u] = tile

    rows = lax.broadcasted_iota(jnp.int32, (32, 1), 0) + lead

    def cols(n):
        return lax.broadcasted_iota(jnp.int32, (32, n), 1)

    g1[z] = s1[z]
    part_recv_wait(0)
    gram1 = jnp.where(rows == cols(512), jnp.broadcast_to(ss_tot[...], (32, 512)), summed(0, 4))
    w1 = weigh(gram1, ss_tot[...], s * 512, cols(512) >= lead)
    pack(w1, p1)

    def t1_copy(t):
        return rcopy(p1.at[t], t1.at[z], t_send.at[0, t], t_recv1.at[z], {"ind": t})

    def span(lo, hi, body):
        def step(t, carry):
            @pl.when((t >= lo) & (t < hi))
            def _():
                body(t)
            return carry
        lax.fori_loop(0, nz, step, 0)

    span(z + 1, nz, lambda t: t1_copy(t).start())

    side_l.wait_send()
    side_r.wait_send()
    side_l.wait_recv()
    side_r.wait_recv()
    g2[z] = s2[z]
    part_recv_wait(1)
    w2 = weigh(summed(1, 2), ss_side[1][:, 0:256], (s + 1) * 512, cols(256) <= rows)
    pack(w2, p2)

    def t2_copy(t):
        return rcopy(p2.at[t], t2.at[z], t_send.at[1, t], t_recv2.at[z], {"snp": right, "ind": t})

    span(0, jnp.minimum(z + 1, 8), lambda t: t2_copy(t).start())

    @pl.when(z >= 8)
    def _():
        g3[z] = s3[z - 8]
    part_recv_wait(2)
    w3 = weigh(summed(2, 2), ss_side[0][:, 256:512], s * 512 - 256, (cols(256) + 256 >= rows) & (z >= 8))
    pack(w3, p3)

    def t3_copy(t):
        return rcopy(p3.at[t - 8], t3.at[z - 8], t_send.at[2, t], t_recv3.at[z - 8], {"snp": left, "ind": t})

    t3_first = jnp.where(z >= 8, z, nz)
    span(t3_first, nz, lambda t: t3_copy(t).start())

    a_copy.wait()
    ann_l.wait_recv()
    ann_r.wait_recv()
    score = mm(w1.astype(BF16), a_own[...])
    score = score + mm(w2.astype(BF16), a_next[0:256, :])
    score = score + mm(w3.astype(BF16), a_prev[256:512, :])

    def t_recv_wait(buf, sems, base, i):
        rcopy(buf.at[i - base], buf.at[i - base], t_send.at[0, i], sems.at[i - base], {"ind": i}).wait_recv()

    span(0, z, lambda i: t_recv_wait(t1, t_recv1, 0, i))
    span(jnp.where(z < 8, z, nz), nz, lambda i: t_recv_wait(t2, t_recv2, 0, i))
    span(8, jnp.where(z >= 8, z + 1, 0), lambda i: t_recv_wait(t3, t_recv3, 8, i))

    def spread(buf, lo, hi, base):
        n = buf.shape[0]
        shape = (n, 4, 8, 128)
        tiles = jnp.broadcast_to(buf[...].reshape(n, 1, 8, 128), shape)
        src = lax.broadcasted_iota(jnp.int32, shape, 0) + base
        v = lax.broadcasted_iota(jnp.int32, shape, 1)
        ln = lax.broadcasted_iota(jnp.int32, shape, 3) // 32
        keep = (ln == v) & (src >= lo) & (src < hi)
        return jnp.where(keep, tiles, 0.0).reshape(n * 32, 128).astype(BF16)

    folded = tdot(spread(t1, 0, z, 0), a_own[...])
    folded = folded + tdot(spread(t2, jnp.where(z < 8, z, nz), nz, 0), a_prev[...])
    folded = folded + tdot(spread(t3, 8, jnp.where(z >= 8, z + 1, 0), 8), a_next[256:512, :])
    for v in range(4):
        score = score + folded[32 * v:32 * v + 32, :]
    out[...] = score

    h_left.wait_send()
    h_right.wait_send()
    ann_l.wait_send()
    ann_r.wait_send()
    each_peer(lambda d: ss_copy(d).wait_send())
    for k in range(3):
        part_send_wait(k)
    span(z + 1, nz, lambda t: t1_copy(t).wait_send())
    span(0, jnp.minimum(z + 1, 8), lambda t: t2_copy(t).wait_send())
    span(t3_first, nz, lambda t: t3_copy(t).wait_send())


def per_device(count_all, snps, genotypes, annotations, window_start, window_end):
    dma = pltpu.SemaphoreType.DMA
    vm = pltpu.VMEM
    any_spec = pl.BlockSpec(memory_space=pl.ANY)
    vmem_spec = pl.BlockSpec(memory_space=pltpu.VMEM)
    return pl.pallas_call(
        functools.partial(kernel, count_all, snps),
        out_shape=jax.ShapeDtypeStruct((32, 512), F32),
        in_specs=[any_spec, any_spec, vmem_spec, vmem_spec],
        out_specs=vmem_spec,
        scratch_shapes=[
            vm((2048, 512), BF16), vm((2048, 256), BF16), vm((2048, 256), BF16),
            vm((512, 512), BF16), vm((512, 512), BF16), vm((512, 512), BF16),
            vm((16, 4, 32, 128), BF16), vm((16, 2, 32, 128), BF16), vm((8, 2, 32, 128), BF16),
            vm((16, 4, 32, 128), BF16), vm((16, 2, 32, 128), BF16), vm((16, 2, 32, 128), BF16),
            vm((1, 512), F32), vm((16, 1, 512), F32), vm((1, 512), F32), vm((2, 1, 512), F32),
            vm((16, 8, 128), F32), vm((8, 8, 128), F32), vm((8, 8, 128), F32),
            vm((16, 8, 128), F32), vm((16, 8, 128), F32), vm((8, 8, 128), F32),
            dma, dma, dma((4,)), dma((4,)), pltpu.SemaphoreType.REGULAR((3,)),
            dma((16,)), dma((16,)), dma((2,)), dma((2,)),
            dma((3, 16)), dma((16,)), dma((16,)), dma((16,)),
            dma((3, 16)), dma((16,)), dma((16,)), dma((8,)),
        ],
        compiler_params=pltpu.CompilerParams(
            collective_id=0, has_side_effects=True, vmem_limit_bytes=48 * 1024 * 1024),
        name="ld_scores",
    )(genotypes, annotations, window_start.reshape(1, 32), window_end.reshape(1, 32))


def solution(mesh):
    snps, groups = mesh.shape["snp"], mesh.shape["ind"]
    body = functools.partial(per_device, float(2048 * groups), snps)
    in_specs = (P("ind", "snp"), P("snp", None), P(("snp", "ind")), P(("snp", "ind")))
    return jax.shard_map(
        body, mesh=mesh, in_specs=in_specs, out_specs=P(("snp", "ind"), None), check_vma=False)
```

time: 140 us -> 70.1 us (0.50)
  Pallas kernels: 0 us -> 64.4 us
  waiting for transfers between devices: 57.2 us -> 0 us
  blocking collectives: 35.9 us -> 0 us
  starting transfers between devices: 15.5 us -> 0 us
  between operations: 13.5 us -> 0.01 us
  matrix products: 5 us -> 0 us
  other arithmetic: 4.17 us -> 0 us
  local copies, waits for them, and re-layouts: 7.77 us -> 4.57 us
    pallas_call x0 -> x1, Pallas kernels: none -> 64.4 us  [per_device(): pl.pallas_call(functools.partial(kernel, count_all, snps), out_shape=jax....]
    all_gather x1 -> x0, blocking collectives: 35.9 us -> none  [gathered_total(): parts = lax.all_gather(array, axis)]
    unnamed x2 -> x0, waiting for transfers between devices: 33.6 us -> none
    ppermute x4 -> x0, waiting for transfers between devices: 23.5 us -> none  [the longest x2 22 us: extended(): lax.ppermute(tail, axis, [(i, (i + 1) % count) for i in range(ends)])]
    ppermute x4 -> x0, starting transfers between devices: 15.5 us -> none  [the longest x2 11.6 us: extended(): lax.ppermute(head, axis, [((i + 1) % count, i) for i in range(ends)])]
    dot_general x2 -> x0, matrix products: 5 us -> none  [the longest x1 3.46 us: transposed_product(): lax.dot_general(left, right, (((0,), (0,)), ((), ())), preferred_element_...]
    reduce_sum x2 -> x0, other arithmetic: 4.16 us -> none  [the longest x1 4.1 us: column_squares(): return jnp.sum(widened * widened, axis=0)]
    unnamed x17 -> x9, local copies, waits for them, and re-layouts: 7.55 us -> 4.57 us
  transfers between devices with their start and end apart: 5 -> 0, of which waited for: 3 -> 0; matrix products, arithmetic and copies ran while one was open for 4% -> 0% of each run, Pallas kernels for 0% -> 0%
where the time goes in v1:
time: 70.1 us; the launch traced here: 69 us
  Pallas kernels  64.4 us (92%)
  local copies, waits for them, and re-layouts  4.57 us (7%)
    pallas_call x1, Pallas kernels, per_device(): pl.pallas_call(functools.partial(kernel, count_all, snps), out_shape=jax....  64.4 us
    unnamed x9, local copies, waits for them, and re-layouts  4.57 us

profile of v1, /device:TPU:24, one launch (start us, length us, event | category | flops | bytes accessed | tf_op | source)
XLA Modules:
  0.0 69.0 jit_solution(9237833250478431604)
XLA Ops:
  0.0 0.0 copy-start
  0.0 1.6 %copy-done = bf16[2048,512]{1,0:T(8,128)(2,1)S(1)} copy-done((bf16[2048,512]{1,0:T(8,128)(2,1)S(1)}, bf16[2048,512]{1,0:T(8,128)(2,1)}, u32[]{:S(2)}) %copy-start) | copy-done | bytes 2097176
  1.6 0.0 copy-start.1
  1.6 1.0 %copy-done.1 = bf16[512,512]{1,0:T(8,128)(2,1)S(1)} copy-done((bf16[512,512]{1,0:T(8,128)(2,1)S(1)}, bf16[512,512]{1,0:T(8,128)(2,1)}, u32[]{:S(2)}) %copy-start.1) | copy-done | bytes 524312
  2.6 0.0 copy-start.2
  2.6 0.7 copy-done.2
  3.3 0.0 copy-start.3
  3.3 0.7 copy-done.3
  3.9 64.4 %ld_scores.1 = f32[32,512]{1,0:T(8,128)S(1)} custom-call(bf16[2048,512]{1,0:T(8,128)(2,1)S(1)} %copy-done, bf16[512,512]{1,0:T(8,128)(2,1)S(1)} %copy-done.1, s32[1,32]{1,0:T(1,128)S(1)} %bitcast.2, s32[1,32]{1,0:T(1,128)S(1)} %bitcast.3), custom_call_target="tpu_custom_call" | custom-call | tf_op jit(solution)/shard_map/ld_scores/pallas_call | solution.py:334
  68.4 0.6 copy.6
Async XLA Ops:
  0.0 1.6 %copy-start = (bf16[2048,512]{1,0:T(8,128)(2,1)S(1)}, bf16[2048,512]{1,0:T(8,128)(2,1)}, u32[]{:S(2)}) copy-start(bf16[2048,512]{1,0:T(8,128)(2,1)} %geno.1) | copy-start | bytes 6291460
  1.6 1.0 %copy-start.1 = (bf16[512,512]{1,0:T(8,128)(2,1)S(1)}, bf16[512,512]{1,0:T(8,128)(2,1)}, u32[]{:S(2)}) copy-start(bf16[512,512]{1,0:T(8,128)(2,1)} %annot.1) | copy-start | bytes 1572868
  2.6 0.7 copy-start.2
  3.3 0.7 copy-start.3

commit v2 on v1

--- a/solution.py
+++ b/solution.py
@@ -23,13 +23,13 @@
     return lax.rsqrt(jnp.where(v > 0.0, v, 1.0))
 
 
-def kernel(count_all, snps, geno, annot, first, last, out,
+def kernel(count_all, snps, geno, annot, first_h, last_h, out,
            x_v, l0, r1, a_own, a_prev, a_next,
-           s1, s2, s3, g1, g2, g3, ss_own, ss_all, ss_tot, ss_side,
+           s1, s2, s3, f1, f2, f3, c1, c2, c3, k1, k2, k3, g1, g2, g3, o1, o2, o3, ss_own, ss_all, ss_tot, ss_side,
            p1, p2, p3, t1, t2, t3,
-           x_sem, a_sem, halo_send, halo_recv, ring,
+           first, last, win_sem, x_sem, a_sem, halo_send, halo_recv, ring,
            ss_send, ss_recv, side_send, side_recv,
-           g_send, g_recv1, g_recv2, g_recv3, t_send, t_recv1, t_recv2, t_recv3):
+           c_send, c_recv, g_send, g_recv, t_send, t_recv1, t_recv2, t_recv3):
     s = lax.axis_index("snp")
     z = lax.axis_index("ind")
     ns, nz = snps, 16
@@ -50,6 +50,10 @@
     x_copy.start()
     a_copy = pltpu.make_async_copy(annot, a_own, a_sem)
     a_copy.start()
+    f_copy = pltpu.make_async_copy(first_h, first, win_sem.at[0])
+    e_copy = pltpu.make_async_copy(last_h, last, win_sem.at[1])
+    f_copy.start()
+    e_copy.start()
 
     barrier = pltpu.get_barrier_semaphore()
     signal(barrier, {"snp": left})
@@ -73,110 +77,152 @@
     eye = (lax.broadcasted_iota(jnp.int32, (256, 256), 0)
            == lax.broadcasted_iota(jnp.int32, (256, 256), 1))
 
+    def ss_copy(d):
+        dest = lax.rem(z + d, nz)
+        return rcopy(ss_own, ss_all.at[z], ss_send.at[d], ss_recv.at[z], {"ind": dest})
+
+    def each_peer(body):
+        def step(d, carry):
+            body(d)
+            return carry
+        lax.fori_loop(1, nz, step, 0)
+
+    def span(lo, hi, body, top=16):
+        def step(t, carry):
+            @pl.when((t >= lo) & (t < hi))
+            def _():
+                body(t)
+            return carry
+        lax.fori_loop(0, top, step, 0)
+
+    def eight(first_e, body):
+        def step(e, carry):
+            body(e)
+            return carry
+        lax.fori_loop(first_e, 8, step, 0)
+
+    even_z = lax.rem(z, 2) == 0
+    toward = (jnp.where(even_z, 1, -1), jnp.where(even_z, -1, 1), jnp.where(even_z, -1, 1))
+    lows = (0, 0, 8)
+
+    def pieces(k, t, act):
+        if k == 0:
+            cases = [((t // 4) == g, g, 4 - g) for g in range(4)]
+        elif k == 1:
+            cases = [(t < 4, 0, 1), (t >= 4, 0, 2)]
+        else:
+            cases = [((t >= 8) & (t < 12), 0, 2), (t >= 12, 1, 1)]
+        for hit, start, size in cases:
+            @pl.when(hit)
+            def _(start=start, size=size):
+                act(pl.ds(start, size))
+
+    sends, wides, gives, sums, ends, owns = (s1, s2, s3), (f1, f2, f3), (c1, c2, c3), (k1, k2, k3), (g1, g2, g3), (o1, o2, o3)
+
+    def give_copy(k, t, part):
+        i = t - lows[k]
+        return rcopy(sends[k].at[i, part], gives[k].at[i, part], c_send.at[k, t], c_recv.at[k, t],
+                     {"ind": zpeer(toward[k])})
+
+    def give(k):
+        def body(e):
+            t = zpeer(toward[k] * (e + 1))
+            pieces(k, t, lambda part: give_copy(k, t, part).start())
+        eight(0, body)
+
+    def give_wait(k):
+        def body(e):
+            t = zpeer(toward[k] * (e + 1))
+            pieces(k, t, lambda part: give_copy(k, t, part).wait_send())
+        eight(0, body)
+
+    def end_copy(k, e, t, part):
+        return rcopy(sums[k].at[t - lows[k], part], ends[k].at[e, part], g_send.at[k, e], g_recv.at[k, e], {"ind": t})
+
+    def combine(k):
+        def body(e):
+            t = zpeer(-toward[k] * e)
+            i = t - lows[k]
+            pieces(k, t, lambda part: give_copy(k, t, part).wait_recv())
+
+            def add():
+                total = wides[k][i] + gives[k][i].astype(F32)
+
+                @pl.when(e == 0)
+                def _():
+                    owns[k][...] = total
+
+                @pl.when(e > 0)
+                def _():
+                    sums[k][i] = total.astype(BF16)
+            if lows[k]:
+                pl.when(t >= lows[k])(add)
+            else:
+                add()
+
+        eight(0, body)
+
+        def send(e):
+            t = zpeer(-toward[k] * e)
+            pieces(k, t, lambda part: end_copy(k, e, t, part).start())
+        eight(1, send)
+
+    def end_send_wait(k):
+        def body(e):
+            t = zpeer(-toward[k] * e)
+            pieces(k, t, lambda part: end_copy(k, e, t, part).wait_send())
+        eight(1, body)
+
+    def end_recv_wait(k):
+        def body(e):
+            pieces(k, z, lambda part: rcopy(
+                ends[k].at[e, part], ends[k].at[e, part], g_send.at[k, e], g_recv.at[k, e],
+                {"ind": zpeer(toward[k])}).wait_recv())
+        eight(1, body)
+
+    def keep_blocks(k, gram, rows_at, block_at):
+        n = gram.shape[0] // 32
+        for b in range(gram.shape[1] // 128):
+            tile = gram[:, 128 * b:128 * b + 128].reshape(n, 32, 128)
+            wides[k][rows_at:rows_at + n, block_at + b] = tile
+            sends[k][rows_at:rows_at + n, block_at + b] = tile.astype(BF16)
+
+    def next_part():
+        h_left.wait_recv()
+        keep_blocks(1, tdot(x_v[...], l0[...]), 0, 0)
+        give(1)
+
+    def prev_part():
+        h_right.wait_recv()
+        keep_blocks(2, tdot(x_v[:, 256:512], r1[...]), 0, 0)
+        give(2)
+
+    odd = lax.rem(s, 2) == 1
+
+    def either(if_odd, if_even):
+        pl.when(odd)(if_odd)
+        pl.when(jnp.logical_not(odd))(if_even)
+
     x_copy.wait()
     m_lo = tdot(x_v[:, 0:256], x_v[...])
-    for b in range(4):
-        s1[0:8, b] = m_lo[:, 128 * b:128 * b + 128].reshape(8, 32, 128).astype(BF16)
+    keep_blocks(0, m_lo, 0, 0)
     ss_own[:, 0:256] = jnp.sum(jnp.where(eye, m_lo[:, 0:256], 0.0), axis=0, keepdims=True)
     pl.semaphore_wait(ring.at[0], 2)
     signal(ring.at[1], {"ind": zpeer(2)})
     signal(ring.at[1], {"ind": zpeer(-2)})
     m_hi = tdot(x_v[:, 256:512], x_v[:, 256:512])
-    for b in range(2):
-        s1[8:16, 2 + b] = m_hi[:, 128 * b:128 * b + 128].reshape(8, 32, 128).astype(BF16)
+    keep_blocks(0, m_hi, 8, 2)
+    give(0)
     ss_own[:, 256:512] = jnp.sum(jnp.where(eye, m_hi, 0.0), axis=0, keepdims=True)
     pl.semaphore_wait(ring.at[1], 2)
     signal(ring.at[2], {"ind": zpeer(4)})
     signal(ring.at[2], {"ind": zpeer(-4)})
+    either(prev_part, next_part)
     pl.semaphore_wait(ring.at[2], 2)
-
-    def ss_copy(d):
-        dest = lax.rem(z + d, nz)
-        return rcopy(ss_own, ss_all.at[z], ss_send.at[d], ss_recv.at[z], {"ind": dest})
-
-    def each_peer(body):
-        def step(d, carry):
-            body(d)
-            return carry
-        lax.fori_loop(1, nz, step, 0)
-
     each_peer(lambda d: ss_copy(d).start())
-
-    def g1_pieces(i, act):
-        for g in range(4):
-            @pl.when(i // 4 == g)
-            def _():
-                act(pl.ds(g, 4 - g))
-
-    def g2_pieces(i, act):
-        @pl.when(i < 4)
-        def _():
-            act(pl.ds(0, 1))
-
-        @pl.when(i >= 4)
-        def _():
-            act(pl.ds(0, 2))
-
-    def g3_pieces(i, act):
-        @pl.when((i >= 8) & (i < 12))
-        def _():
-            act(pl.ds(0, 2))
-
-        @pl.when(i >= 12)
-        def _():
-            act(pl.ds(1, 1))
-
-    groups = ((s1, g1, g_recv1, g1_pieces, 0), (s2, g2, g_recv2, g2_pieces, 0), (s3, g3, g_recv3, g3_pieces, 8))
-
-    def part_copy(k, d, part):
-        src, dst, rsem, _, base = groups[k]
-        dest = lax.rem(z + d, nz)
-        return rcopy(src.at[dest - base, part], dst.at[z, part], g_send.at[k, d], rsem.at[z], {"ind": dest})
-
-    def part_start(k):
-        def body(d):
-            groups[k][3](lax.rem(z + d, nz), lambda part: part_copy(k, d, part).start())
-        each_peer(body)
-
-    def part_send_wait(k):
-        def body(d):
-            groups[k][3](lax.rem(z + d, nz), lambda part: part_copy(k, d, part).wait_send())
-        each_peer(body)
-
-    def part_recv_wait(k):
-        src, dst, rsem, pieces, base = groups[k]
-
-        def body(d):
-            origin = lax.rem(z + d, nz)
-            pieces(z, lambda part: rcopy(
-                dst.at[origin, part], dst.at[origin, part], g_send.at[k, d], rsem.at[origin], {"ind": origin}).wait_recv())
-        each_peer(body)
-
-    part_start(0)
-
-    def next_part():
-        h_left.wait_recv()
-        m2 = tdot(x_v[...], l0[...])
-        for b in range(2):
-            s2[:, b] = m2[:, 128 * b:128 * b + 128].reshape(16, 32, 128).astype(BF16)
-        part_start(1)
-
-    def prev_part():
-        h_right.wait_recv()
-        m3 = tdot(x_v[:, 256:512], r1[...])
-        for b in range(2):
-            s3[:, b] = m3[:, 128 * b:128 * b + 128].reshape(8, 32, 128).astype(BF16)
-        part_start(2)
-
-    @pl.when(lax.rem(s, 2) == 1)
-    def _():
-        prev_part()
-
-    next_part()
-
-    @pl.when(lax.rem(s, 2) == 0)
-    def _():
-        prev_part()
+    combine(0)
+    either(lambda: combine(2), lambda: combine(1))
+    either(next_part, prev_part)
 
     ss_all[z] = ss_own[...]
 
@@ -189,6 +235,7 @@
     side_r = rcopy(ss_tot, ss_side.at[0], side_send.at[1], side_recv.at[0], {"snp": right})
     side_l.start()
     side_r.start()
+    either(lambda: combine(1), lambda: combine(2))
 
     def column(row, offset):
         n = row.shape[1]
@@ -198,6 +245,8 @@
                        axis=1, keepdims=True)
 
     lead = z * 32
+    f_copy.wait()
+    e_copy.wait()
     low = column(first[...], 0)
     high = column(last[...], 0)
     row_scale = safe_rsqrt(column(ss_tot[...], lead))
@@ -212,10 +261,9 @@
         return jnp.where(inside, adjusted, 0.0).astype(BF16).astype(F32)
 
     def summed(k, width):
-        src, dst, _, pieces, base = groups[k]
-        total = dst[0].astype(F32)
-        for i in range(1, nz):
-            total = total + dst[i].astype(F32)
+        total = owns[k][...]
+        for e in range(1, 8):
+            total = total + ends[k][e].astype(F32)
         return jnp.concatenate([total[b] for b in range(width)], axis=1)
 
     lane = lax.broadcasted_iota(jnp.int32, (8, 128), 1) // 32
@@ -237,22 +285,13 @@
     def cols(n):
         return lax.broadcasted_iota(jnp.int32, (32, n), 1)
 
-    g1[z] = s1[z]
-    part_recv_wait(0)
+    end_recv_wait(0)
     gram1 = jnp.where(rows == cols(512), jnp.broadcast_to(ss_tot[...], (32, 512)), summed(0, 4))
     w1 = weigh(gram1, ss_tot[...], s * 512, cols(512) >= lead)
     pack(w1, p1)
 
     def t1_copy(t):
         return rcopy(p1.at[t], t1.at[z], t_send.at[0, t], t_recv1.at[z], {"ind": t})
-
-    def span(lo, hi, body):
-        def step(t, carry):
-            @pl.when((t >= lo) & (t < hi))
-            def _():
-                body(t)
-            return carry
-        lax.fori_loop(0, nz, step, 0)
 
     span(z + 1, nz, lambda t: t1_copy(t).start())
 
@@ -260,8 +299,7 @@
     side_r.wait_send()
     side_l.wait_recv()
     side_r.wait_recv()
-    g2[z] = s2[z]
-    part_recv_wait(1)
+    end_recv_wait(1)
     w2 = weigh(summed(1, 2), ss_side[1][:, 0:256], (s + 1) * 512, cols(256) <= rows)
     pack(w2, p2)
 
@@ -270,10 +308,7 @@
 
     span(0, jnp.minimum(z + 1, 8), lambda t: t2_copy(t).start())
 
-    @pl.when(z >= 8)
-    def _():
-        g3[z] = s3[z - 8]
-    part_recv_wait(2)
+    end_recv_wait(2)
     w3 = weigh(summed(2, 2), ss_side[0][:, 256:512], s * 512 - 256, (cols(256) + 256 >= rows) & (z >= 8))
     pack(w3, p3)
 
@@ -320,7 +355,8 @@
     ann_r.wait_send()
     each_peer(lambda d: ss_copy(d).wait_send())
     for k in range(3):
-        part_send_wait(k)
+        give_wait(k)
+        end_send_wait(k)
     span(z + 1, nz, lambda t: t1_copy(t).wait_send())
     span(0, jnp.minimum(z + 1, 8), lambda t: t2_copy(t).wait_send())
     span(t3_first, nz, lambda t: t3_copy(t).wait_send())
@@ -329,28 +365,30 @@
 def per_device(count_all, snps, genotypes, annotations, window_start, window_end):
     dma = pltpu.SemaphoreType.DMA
     vm = pltpu.VMEM
-    any_spec = pl.BlockSpec(memory_space=pl.ANY)
+    any_spec = pl.BlockSpec(memory_space=pltpu.HBM)
     vmem_spec = pl.BlockSpec(memory_space=pltpu.VMEM)
     return pl.pallas_call(
         functools.partial(kernel, count_all, snps),
         out_shape=jax.ShapeDtypeStruct((32, 512), F32),
-        in_specs=[any_spec, any_spec, vmem_spec, vmem_spec],
+        in_specs=[any_spec, any_spec, any_spec, any_spec],
         out_specs=vmem_spec,
         scratch_shapes=[
             vm((2048, 512), BF16), vm((2048, 256), BF16), vm((2048, 256), BF16),
             vm((512, 512), BF16), vm((512, 512), BF16), vm((512, 512), BF16),
-            vm((16, 4, 32, 128), BF16), vm((16, 2, 32, 128), BF16), vm((8, 2, 32, 128), BF16),
-            vm((16, 4, 32, 128), BF16), vm((16, 2, 32, 128), BF16), vm((16, 2, 32, 128), BF16),
+            *[vm((n, b, 32, 128), kind) for kind in (BF16, F32, BF16, BF16) for n, b in ((16, 4), (16, 2), (8, 2))],
+            *[vm((8, b, 32, 128), BF16) for b in (4, 2, 2)],
+            *[vm((b, 32, 128), F32) for b in (4, 2, 2)],
             vm((1, 512), F32), vm((16, 1, 512), F32), vm((1, 512), F32), vm((2, 1, 512), F32),
             vm((16, 8, 128), F32), vm((8, 8, 128), F32), vm((8, 8, 128), F32),
             vm((16, 8, 128), F32), vm((16, 8, 128), F32), vm((8, 8, 128), F32),
+            vm((1, 32), jnp.int32), vm((1, 32), jnp.int32), dma((2,)),
             dma, dma, dma((4,)), dma((4,)), pltpu.SemaphoreType.REGULAR((3,)),
             dma((16,)), dma((16,)), dma((2,)), dma((2,)),
-            dma((3, 16)), dma((16,)), dma((16,)), dma((16,)),
+            dma((3, 16)), dma((3, 16)), dma((3, 8)), dma((3, 8)),
             dma((3, 16)), dma((16,)), dma((16,)), dma((8,)),
         ],
         compiler_params=pltpu.CompilerParams(
-            collective_id=0, has_side_effects=True, vmem_limit_bytes=48 * 1024 * 1024),
+            collective_id=0, has_side_effects=True, vmem_limit_bytes=67043328),
         name="ld_scores",
     )(genotypes, annotations, window_start.reshape(1, 32), window_end.reshape(1, 32))
 

time: 70.1 us -> 57.6 us (0.82)
  the two profiles are of different devices: /device:TPU:24 before, /device:TPU:2 now
where the time goes in v2:
time: 57.6 us; the launch traced here: 57.5 us
  Pallas kernels  56 us (97%)
  local copies, waits for them, and re-layouts  1.47 us (3%)
    pallas_call x1, Pallas kernels, per_device(): pl.pallas_call(functools.partial(kernel, count_all, snps), out_shape=jax....  56 us
    unnamed x1, local copies, waits for them, and re-layouts  1.47 us

profile of v2, /device:TPU:2, one launch (start us, length us, event | category | flops | bytes accessed | tf_op | source)
XLA Modules:
  0.0 57.5 jit_solution(12411160882336168687)
XLA Ops:
  0.0 56.0 %ld_scores.1 = f32[32,512]{1,0:T(8,128)} custom-call(bf16[2048,512]{1,0:T(8,128)(2,1)} %geno.1, bf16[512,512]{1,0:T(8,128)(2,1)} %annot.1, s32[1,32]{1,0:T(1,128)} %bitcast.2, s32[1,32]{1,0:T(1,128)} %bitcast.3), custom_call_target="tpu_custom_call" | custom-call | tf_op jit(solution)/shard_map/ld_scores/pallas_call | solution.py:370
  56.0 1.5 %copy.6 = f32[32,512]{1,0:T(8,128)} copy(f32[32,512]{1,0:T(8,128)} %ld_scores.1) | data formatting | bytes 131072

commit v3 on v2

--- a/solution.py
+++ b/solution.py
@@ -25,7 +25,7 @@
 
 def kernel(count_all, snps, geno, annot, first_h, last_h, out,
            x_v, l0, r1, a_own, a_prev, a_next,
-           s1, s2, s3, f1, f2, f3, c1, c2, c3, k1, k2, k3, g1, g2, g3, o1, o2, o3, ss_own, ss_all, ss_tot, ss_side,
+           s1, s2, s3, f1, f2, f3, c1, c2, c3, k1, k2, k3, g1, g2, g3, o1, o2, o3, score_v, folded_v, ss_own, ss_all, ss_tot, ss_side,
            p1, p2, p3, t1, t2, t3,
            first, last, win_sem, x_sem, a_sem, halo_send, halo_recv, ring,
            ss_send, ss_recv, side_send, side_recv,
@@ -95,11 +95,11 @@
             return carry
         lax.fori_loop(0, top, step, 0)
 
-    def eight(first_e, body):
+    def eight(first_e, body, end_e=8):
         def step(e, carry):
             body(e)
             return carry
-        lax.fori_loop(first_e, 8, step, 0)
+        lax.fori_loop(first_e, end_e, step, 0)
 
     even_z = lax.rem(z, 2) == 0
     toward = (jnp.where(even_z, 1, -1), jnp.where(even_z, -1, 1), jnp.where(even_z, -1, 1))
@@ -139,8 +139,9 @@
     def end_copy(k, e, t, part):
         return rcopy(sums[k].at[t - lows[k], part], ends[k].at[e, part], g_send.at[k, e], g_recv.at[k, e], {"ind": t})
 
-    def combine(k):
-        def body(e):
+    def combine(k, near=0, far=8):
+        def body(n):
+            e = near + far - 1 - n
             t = zpeer(-toward[k] * e)
             i = t - lows[k]
             pieces(k, t, lambda part: give_copy(k, t, part).wait_recv())
@@ -160,12 +161,11 @@
             else:
                 add()
 
-        eight(0, body)
-
-        def send(e):
-            t = zpeer(-toward[k] * e)
-            pieces(k, t, lambda part: end_copy(k, e, t, part).start())
-        eight(1, send)
+            def go():
+                pieces(k, t, lambda part: end_copy(k, e, t, part).start())
+            pl.when(e > 0)(go)
+
+        eight(near, body, far)
 
     def end_send_wait(k):
         def body(e):
@@ -203,20 +203,20 @@
         pl.when(odd)(if_odd)
         pl.when(jnp.logical_not(odd))(if_even)
 
+    pl.semaphore_wait(ring.at[0], 2)
+    signal(ring.at[1], {"ind": zpeer(2)})
+    signal(ring.at[1], {"ind": zpeer(-2)})
     x_copy.wait()
     m_lo = tdot(x_v[:, 0:256], x_v[...])
     keep_blocks(0, m_lo, 0, 0)
     ss_own[:, 0:256] = jnp.sum(jnp.where(eye, m_lo[:, 0:256], 0.0), axis=0, keepdims=True)
-    pl.semaphore_wait(ring.at[0], 2)
-    signal(ring.at[1], {"ind": zpeer(2)})
-    signal(ring.at[1], {"ind": zpeer(-2)})
+    pl.semaphore_wait(ring.at[1], 2)
+    signal(ring.at[2], {"ind": zpeer(4)})
+    signal(ring.at[2], {"ind": zpeer(-4)})
     m_hi = tdot(x_v[:, 256:512], x_v[:, 256:512])
     keep_blocks(0, m_hi, 8, 2)
     give(0)
     ss_own[:, 256:512] = jnp.sum(jnp.where(eye, m_hi, 0.0), axis=0, keepdims=True)
-    pl.semaphore_wait(ring.at[1], 2)
-    signal(ring.at[2], {"ind": zpeer(4)})
-    signal(ring.at[2], {"ind": zpeer(-4)})
     either(prev_part, next_part)
     pl.semaphore_wait(ring.at[2], 2)
     each_peer(lambda d: ss_copy(d).start())
@@ -278,7 +278,7 @@
                     if shift:
                         piece = pltpu.roll(piece, shift, 1)
                     tile = jnp.where(lane == v, piece, tile)
-                buf[4 * b + u] = tile
+                buf[4 * b + u] = tile.astype(BF16)
 
     rows = lax.broadcasted_iota(jnp.int32, (32, 1), 0) + lead
 
@@ -299,55 +299,34 @@
     side_r.wait_send()
     side_l.wait_recv()
     side_r.wait_recv()
-    end_recv_wait(1)
-    w2 = weigh(summed(1, 2), ss_side[1][:, 0:256], (s + 1) * 512, cols(256) <= rows)
-    pack(w2, p2)
-
     def t2_copy(t):
         return rcopy(p2.at[t], t2.at[z], t_send.at[1, t], t_recv2.at[z], {"snp": right, "ind": t})
 
-    span(0, jnp.minimum(z + 1, 8), lambda t: t2_copy(t).start())
-
-    end_recv_wait(2)
-    w3 = weigh(summed(2, 2), ss_side[0][:, 256:512], s * 512 - 256, (cols(256) + 256 >= rows) & (z >= 8))
-    pack(w3, p3)
-
     def t3_copy(t):
         return rcopy(p3.at[t - 8], t3.at[z - 8], t_send.at[2, t], t_recv3.at[z - 8], {"snp": left, "ind": t})
 
     t3_first = jnp.where(z >= 8, z, nz)
-    span(t3_first, nz, lambda t: t3_copy(t).start())
-
     a_copy.wait()
     ann_l.wait_recv()
     ann_r.wait_recv()
-    score = mm(w1.astype(BF16), a_own[...])
-    score = score + mm(w2.astype(BF16), a_next[0:256, :])
-    score = score + mm(w3.astype(BF16), a_prev[256:512, :])
-
-    def t_recv_wait(buf, sems, base, i):
-        rcopy(buf.at[i - base], buf.at[i - base], t_send.at[0, i], sems.at[i - base], {"ind": i}).wait_recv()
-
-    span(0, z, lambda i: t_recv_wait(t1, t_recv1, 0, i))
-    span(jnp.where(z < 8, z, nz), nz, lambda i: t_recv_wait(t2, t_recv2, 0, i))
-    span(8, jnp.where(z >= 8, z + 1, 0), lambda i: t_recv_wait(t3, t_recv3, 8, i))
-
-    def spread(buf, lo, hi, base):
-        n = buf.shape[0]
-        shape = (n, 4, 8, 128)
-        tiles = jnp.broadcast_to(buf[...].reshape(n, 1, 8, 128), shape)
-        src = lax.broadcasted_iota(jnp.int32, shape, 0) + base
-        v = lax.broadcasted_iota(jnp.int32, shape, 1)
-        ln = lax.broadcasted_iota(jnp.int32, shape, 3) // 32
-        keep = (ln == v) & (src >= lo) & (src < hi)
-        return jnp.where(keep, tiles, 0.0).reshape(n * 32, 128).astype(BF16)
-
-    folded = tdot(spread(t1, 0, z, 0), a_own[...])
-    folded = folded + tdot(spread(t2, jnp.where(z < 8, z, nz), nz, 0), a_prev[...])
-    folded = folded + tdot(spread(t3, 8, jnp.where(z >= 8, z + 1, 0), 8), a_next[256:512, :])
-    for v in range(4):
-        score = score + folded[32 * v:32 * v + 32, :]
-    out[...] = score
+    score_v[...] = mm(w1.astype(BF16), a_own[...])
+
+    def next_own():
+        end_recv_wait(1)
+        w2 = weigh(summed(1, 2), ss_side[1][:, 0:256], (s + 1) * 512, cols(256) <= rows)
+        pack(w2, p2)
+        span(0, jnp.minimum(z + 1, 8), lambda t: t2_copy(t).start())
+        score_v[...] += mm(w2.astype(BF16), a_next[0:256, :])
+
+    def prev_own():
+        end_recv_wait(2)
+        w3 = weigh(summed(2, 2), ss_side[0][:, 256:512], s * 512 - 256, (cols(256) + 256 >= rows) & (z >= 8))
+        pack(w3, p3)
+        span(t3_first, nz, lambda t: t3_copy(t).start())
+        score_v[...] += mm(w3.astype(BF16), a_prev[256:512, :])
+
+    either(prev_own, next_own)
+    either(next_own, prev_own)
 
     h_left.wait_send()
     h_right.wait_send()
@@ -360,6 +339,32 @@
     span(z + 1, nz, lambda t: t1_copy(t).wait_send())
     span(0, jnp.minimum(z + 1, 8), lambda t: t2_copy(t).wait_send())
     span(t3_first, nz, lambda t: t3_copy(t).wait_send())
+
+    def t_recv_wait(buf, sems, base, i):
+        rcopy(buf.at[i - base], buf.at[i - base], t_send.at[0, i], sems.at[i - base], {"ind": i}).wait_recv()
+
+    def spread(buf, lo, hi, base):
+        n = buf.shape[0]
+        shape = (n, 4, 8, 128)
+        tiles = jnp.broadcast_to(buf[...].astype(F32).reshape(n, 1, 8, 128), shape)
+        src = lax.broadcasted_iota(jnp.int32, shape, 0) + base
+        v = lax.broadcasted_iota(jnp.int32, shape, 1)
+        ln = lax.broadcasted_iota(jnp.int32, shape, 3) // 32
+        keep = (ln == v) & (src >= lo) & (src < hi)
+        return jnp.where(keep, tiles, 0.0).reshape(n * 32, 128).astype(BF16)
+
+    span(0, z, lambda i: t_recv_wait(t1, t_recv1, 0, i))
+    folded = tdot(spread(t1, 0, z, 0), a_own[...])
+    folded_v[...] = folded
+    span(jnp.where(z < 8, z, nz), nz, lambda i: t_recv_wait(t2, t_recv2, 0, i))
+    span(8, jnp.where(z >= 8, z + 1, 0), lambda i: t_recv_wait(t3, t_recv3, 8, i))
+    score = score_v[...]
+    folded = folded_v[...]
+    folded = folded + tdot(spread(t2, jnp.where(z < 8, z, nz), nz, 0), a_prev[...])
+    folded = folded + tdot(spread(t3, 8, jnp.where(z >= 8, z + 1, 0), 8), a_next[256:512, :])
+    for v in range(4):
+        score = score + folded[32 * v:32 * v + 32, :]
+    out[...] = score
 
 
 def per_device(count_all, snps, genotypes, annotations, window_start, window_end):
@@ -377,10 +382,10 @@
             vm((512, 512), BF16), vm((512, 512), BF16), vm((512, 512), BF16),
             *[vm((n, b, 32, 128), kind) for kind in (BF16, F32, BF16, BF16) for n, b in ((16, 4), (16, 2), (8, 2))],
             *[vm((8, b, 32, 128), BF16) for b in (4, 2, 2)],
-            *[vm((b, 32, 128), F32) for b in (4, 2, 2)],
+            *[vm((b, 32, 128), F32) for b in (4, 2, 2)], vm((32, 512), F32), vm((128, 512), F32),
             vm((1, 512), F32), vm((16, 1, 512), F32), vm((1, 512), F32), vm((2, 1, 512), F32),
-            vm((16, 8, 128), F32), vm((8, 8, 128), F32), vm((8, 8, 128), F32),
-            vm((16, 8, 128), F32), vm((16, 8, 128), F32), vm((8, 8, 128), F32),
+            vm((16, 8, 128), BF16), vm((8, 8, 128), BF16), vm((8, 8, 128), BF16),
+            vm((16, 8, 128), BF16), vm((16, 8, 128), BF16), vm((8, 8, 128), BF16),
             vm((1, 32), jnp.int32), vm((1, 32), jnp.int32), dma((2,)),
             dma, dma, dma((4,)), dma((4,)), pltpu.SemaphoreType.REGULAR((3,)),
             dma((16,)), dma((16,)), dma((2,)), dma((2,)),

time: 57.6 us -> 54.9 us (0.953)
  the two profiles are of different devices: /device:TPU:2 before, /device:TPU:24 now
where the time goes in v3:
time: 54.9 us; the launch traced here: 54.7 us
  Pallas kernels  53.2 us (97%)
  local copies, waits for them, and re-layouts  1.47 us (3%)
    pallas_call x1, Pallas kernels, per_device(): pl.pallas_call(functools.partial(kernel, count_all, snps), out_shape=jax....  53.2 us
    unnamed x1, local copies, waits for them, and re-layouts  1.47 us

profile of v3, /device:TPU:24, one launch (start us, length us, event | category | flops | bytes accessed | tf_op | source)
XLA Modules:
  0.0 54.7 jit_solution(10523324832125597062)
XLA Ops:
  0.0 53.2 %ld_scores.1 = f32[32,512]{1,0:T(8,128)} custom-call(bf16[2048,512]{1,0:T(8,128)(2,1)} %geno.1, bf16[512,512]{1,0:T(8,128)(2,1)} %annot.1, s32[1,32]{1,0:T(1,128)} %bitcast.2, s32[1,32]{1,0:T(1,128)} %bitcast.3), custom_call_target="tpu_custom_call" | custom-call | tf_op jit(solution)/shard_map/ld_scores/pallas_call | solution.py:375
  53.2 1.5 %copy.6 = f32[32,512]{1,0:T(8,128)} copy(f32[32,512]{1,0:T(8,128)} %ld_scores.1) | data formatting | bytes 131072

commit v4 on v3

--- a/solution.py
+++ b/solution.py
@@ -81,11 +81,11 @@
         dest = lax.rem(z + d, nz)
         return rcopy(ss_own, ss_all.at[z], ss_send.at[d], ss_recv.at[z], {"ind": dest})
 
-    def each_peer(body):
+    def each_peer(body, lo=1, hi=16):
         def step(d, carry):
             body(d)
             return carry
-        lax.fori_loop(1, nz, step, 0)
+        lax.fori_loop(lo, hi, step, 0)
 
     def span(lo, hi, body, top=16):
         def step(t, carry):
@@ -125,8 +125,8 @@
                      {"ind": zpeer(toward[k])})
 
     def give(k):
-        def body(e):
-            t = zpeer(toward[k] * (e + 1))
+        def body(n):
+            t = zpeer(toward[k] * (8 - n))
             pieces(k, t, lambda part: give_copy(k, t, part).start())
         eight(0, body)
 
@@ -217,9 +217,11 @@
     keep_blocks(0, m_hi, 8, 2)
     give(0)
     ss_own[:, 256:512] = jnp.sum(jnp.where(eye, m_hi, 0.0), axis=0, keepdims=True)
+    each_peer(lambda d: ss_copy(d).start(), 1, 5)
+    each_peer(lambda d: ss_copy(d).start(), 12, 16)
     either(prev_part, next_part)
     pl.semaphore_wait(ring.at[2], 2)
-    each_peer(lambda d: ss_copy(d).start())
+    each_peer(lambda d: ss_copy(d).start(), 5, 12)
     combine(0)
     either(lambda: combine(2), lambda: combine(1))
     either(next_part, prev_part)

time: 54.9 us -> 54.4 us (level)
  the two profiles are of different devices: /device:TPU:24 before, /device:TPU:32 now
where the time goes in v4:
time: 54.4 us; the launch traced here: 54.2 us
  Pallas kernels  52.7 us (97%)
  local copies, waits for them, and re-layouts  1.47 us (3%)
    pallas_call x1, Pallas kernels, per_device(): pl.pallas_call(functools.partial(kernel, count_all, snps), out_shape=jax....  52.7 us
    unnamed x1, local copies, waits for them, and re-layouts  1.47 us

profile of v4, /device:TPU:32, one launch (start us, length us, event | category | flops | bytes accessed | tf_op | source)
XLA Modules:
  0.0 54.2 jit_solution(4597576199090697270)
XLA Ops:
  0.0 52.7 %ld_scores.1 = f32[32,512]{1,0:T(8,128)} custom-call(bf16[2048,512]{1,0:T(8,128)(2,1)} %geno.1, bf16[512,512]{1,0:T(8,128)(2,1)} %annot.1, s32[1,32]{1,0:T(1,128)} %bitcast.2, s32[1,32]{1,0:T(1,128)} %bitcast.3), custom_call_target="tpu_custom_call" | custom-call | tf_op jit(solution)/shard_map/ld_scores/pallas_call | solution.py:377
  52.7 1.5 %copy.6 = f32[32,512]{1,0:T(8,128)} copy(f32[32,512]{1,0:T(8,128)} %ld_scores.1) | data formatting | bytes 131072

commit v5 on v4

--- a/solution.py
+++ b/solution.py
@@ -124,10 +124,13 @@
         return rcopy(sends[k].at[i, part], gives[k].at[i, part], c_send.at[k, t], c_recv.at[k, t],
                      {"ind": zpeer(toward[k])})
 
-    def give(k):
+    def give(k, lo=0, hi=16):
         def body(n):
             t = zpeer(toward[k] * (8 - n))
-            pieces(k, t, lambda part: give_copy(k, t, part).start())
+
+            @pl.when((t >= lo) & (t < hi))
+            def _():
+                pieces(k, t, lambda part: give_copy(k, t, part).start())
         eight(0, body)
 
     def give_wait(k):
@@ -209,13 +212,14 @@
     x_copy.wait()
     m_lo = tdot(x_v[:, 0:256], x_v[...])
     keep_blocks(0, m_lo, 0, 0)
+    give(0, 0, 8)
     ss_own[:, 0:256] = jnp.sum(jnp.where(eye, m_lo[:, 0:256], 0.0), axis=0, keepdims=True)
     pl.semaphore_wait(ring.at[1], 2)
     signal(ring.at[2], {"ind": zpeer(4)})
     signal(ring.at[2], {"ind": zpeer(-4)})
     m_hi = tdot(x_v[:, 256:512], x_v[:, 256:512])
     keep_blocks(0, m_hi, 8, 2)
-    give(0)
+    give(0, 8, 16)
     ss_own[:, 256:512] = jnp.sum(jnp.where(eye, m_hi, 0.0), axis=0, keepdims=True)
     each_peer(lambda d: ss_copy(d).start(), 1, 5)
     each_peer(lambda d: ss_copy(d).start(), 12, 16)
@@ -307,7 +311,10 @@
     def t3_copy(t):
         return rcopy(p3.at[t - 8], t3.at[z - 8], t_send.at[2, t], t_recv3.at[z - 8], {"snp": left, "ind": t})
 
-    t3_first = jnp.where(z >= 8, z, nz)
+    t3_first = jnp.where((z >= 8) & (s > 0), z, nz)
+    t2_end = jnp.where(s < ns - 1, jnp.minimum(z + 1, 8), 0)
+    t2_from = jnp.where((z < 8) & (s > 0), z, nz)
+    t3_end = jnp.where((z >= 8) & (s < ns - 1), z + 1, 0)
     a_copy.wait()
     ann_l.wait_recv()
     ann_r.wait_recv()
@@ -317,7 +324,7 @@
         end_recv_wait(1)
         w2 = weigh(summed(1, 2), ss_side[1][:, 0:256], (s + 1) * 512, cols(256) <= rows)
         pack(w2, p2)
-        span(0, jnp.minimum(z + 1, 8), lambda t: t2_copy(t).start())
+        span(0, t2_end, lambda t: t2_copy(t).start())
         score_v[...] += mm(w2.astype(BF16), a_next[0:256, :])
 
     def prev_own():
@@ -339,7 +346,7 @@
         give_wait(k)
         end_send_wait(k)
     span(z + 1, nz, lambda t: t1_copy(t).wait_send())
-    span(0, jnp.minimum(z + 1, 8), lambda t: t2_copy(t).wait_send())
+    span(0, t2_end, lambda t: t2_copy(t).wait_send())
     span(t3_first, nz, lambda t: t3_copy(t).wait_send())
 
     def t_recv_wait(buf, sems, base, i):
@@ -358,12 +365,12 @@
     span(0, z, lambda i: t_recv_wait(t1, t_recv1, 0, i))
     folded = tdot(spread(t1, 0, z, 0), a_own[...])
     folded_v[...] = folded
-    span(jnp.where(z < 8, z, nz), nz, lambda i: t_recv_wait(t2, t_recv2, 0, i))
-    span(8, jnp.where(z >= 8, z + 1, 0), lambda i: t_recv_wait(t3, t_recv3, 8, i))
+    span(t2_from, nz, lambda i: t_recv_wait(t2, t_recv2, 0, i))
+    span(8, t3_end, lambda i: t_recv_wait(t3, t_recv3, 8, i))
     score = score_v[...]
     folded = folded_v[...]
-    folded = folded + tdot(spread(t2, jnp.where(z < 8, z, nz), nz, 0), a_prev[...])
-    folded = folded + tdot(spread(t3, 8, jnp.where(z >= 8, z + 1, 0), 8), a_next[256:512, :])
+    folded = folded + tdot(spread(t2, t2_from, nz, 0), a_prev[...])
+    folded = folded + tdot(spread(t3, 8, t3_end, 8), a_next[256:512, :])
     for v in range(4):
         score = score + folded[32 * v:32 * v + 32, :]
     out[...] = score

time: 54.4 us -> 51.5 us (0.947)
  the two profiles are of different devices: /device:TPU:32 before, /device:TPU:24 now
where the time goes in v5:
time: 51.5 us; the launch traced here: 50.8 us
  Pallas kernels  49.3 us (96%)
  local copies, waits for them, and re-layouts  1.47 us (3%)
    pallas_call x1, Pallas kernels, per_device(): pl.pallas_call(functools.partial(kernel, count_all, snps), out_shape=jax....  49.3 us
    unnamed x1, local copies, waits for them, and re-layouts  1.47 us

profile of v5, /device:TPU:24, one launch (start us, length us, event | category | flops | bytes accessed | tf_op | source)
XLA Modules:
  0.0 50.8 jit_solution(6574936257939611961)
XLA Ops:
  0.0 49.3 %ld_scores.1 = f32[32,512]{1,0:T(8,128)} custom-call(bf16[2048,512]{1,0:T(8,128)(2,1)} %geno.1, bf16[512,512]{1,0:T(8,128)(2,1)} %annot.1, s32[1,32]{1,0:T(1,128)} %bitcast.2, s32[1,32]{1,0:T(1,128)} %bitcast.3), custom_call_target="tpu_custom_call" | custom-call | tf_op jit(solution)/shard_map/ld_scores/pallas_call | solution.py:384
  49.3 1.5 %copy.6 = f32[32,512]{1,0:T(8,128)} copy(f32[32,512]{1,0:T(8,128)} %ld_scores.1) | data formatting | bytes 131072

commit v6 on v5

--- a/solution.py
+++ b/solution.py
@@ -228,7 +228,15 @@
     each_peer(lambda d: ss_copy(d).start(), 5, 12)
     combine(0)
     either(lambda: combine(2), lambda: combine(1))
-    either(next_part, prev_part)
+    has_next, has_prev = s < ns - 1, s > 0
+
+    def where_next(body):
+        pl.when(has_next)(body)
+
+    def where_prev(body):
+        pl.when(has_prev)(body)
+
+    either(lambda: where_next(next_part), lambda: where_prev(prev_part))
 
     ss_all[z] = ss_own[...]
 
@@ -241,7 +249,7 @@
     side_r = rcopy(ss_tot, ss_side.at[0], side_send.at[1], side_recv.at[0], {"snp": right})
     side_l.start()
     side_r.start()
-    either(lambda: combine(1), lambda: combine(2))
+    either(lambda: where_next(lambda: combine(1)), lambda: where_prev(lambda: combine(2)))
 
     def column(row, offset):
         n = row.shape[1]
@@ -335,16 +343,21 @@
         score_v[...] += mm(w3.astype(BF16), a_prev[256:512, :])
 
     either(prev_own, next_own)
-    either(next_own, prev_own)
+    either(lambda: where_next(next_own), lambda: where_prev(prev_own))
 
     h_left.wait_send()
     h_right.wait_send()
     ann_l.wait_send()
     ann_r.wait_send()
     each_peer(lambda d: ss_copy(d).wait_send())
-    for k in range(3):
+    def part_left(k):
         give_wait(k)
         end_send_wait(k)
+    part_left(0)
+    where_next(lambda: part_left(1))
+    where_prev(lambda: part_left(2))
+    pl.when(jnp.logical_not(has_next))(h_left.wait_recv)
+    pl.when(jnp.logical_not(has_prev))(h_right.wait_recv)
     span(z + 1, nz, lambda t: t1_copy(t).wait_send())
     span(0, t2_end, lambda t: t2_copy(t).wait_send())
     span(t3_first, nz, lambda t: t3_copy(t).wait_send())

time: 51.5 us -> 51.5 us (level)
  no operation moved by 1% of the time
where the time goes in v6:
time: 51.5 us; the launch traced here: 50.8 us
  Pallas kernels  49.3 us (96%)
  local copies, waits for them, and re-layouts  1.47 us (3%)
    pallas_call x1, Pallas kernels, per_device(): pl.pallas_call(functools.partial(kernel, count_all, snps), out_shape=jax....  49.3 us
    unnamed x1, local copies, waits for them, and re-layouts  1.47 us

profile of v6, /device:TPU:24, one launch (start us, length us, event | category | flops | bytes accessed | tf_op | source)
XLA Modules:
  0.0 50.8 jit_solution(1276501147941928958)
XLA Ops:
  0.0 49.3 %ld_scores.1 = f32[32,512]{1,0:T(8,128)} custom-call(bf16[2048,512]{1,0:T(8,128)(2,1)} %geno.1, bf16[512,512]{1,0:T(8,128)(2,1)} %annot.1, s32[1,32]{1,0:T(1,128)} %bitcast.2, s32[1,32]{1,0:T(1,128)} %bitcast.3), custom_call_target="tpu_custom_call" | custom-call | tf_op jit(solution)/shard_map/ld_scores/pallas_call | solution.py:397
  49.3 1.5 %copy.6 = f32[32,512]{1,0:T(8,128)} copy(f32[32,512]{1,0:T(8,128)} %ld_scores.1) | data formatting | bytes 131072
